TPU v7x, 256 devices: a whole 4x4x8 slice. The times are simulated.
256 devices in a mesh: seq: 32 (over x, y, core), tp: 8 (over z).
Axes of the slice: x: 4, y: 4, z: 8, core: 2. Of those that a mesh axis runs over, the one named last changes fastest.
Arguments:
- hidden: bfloat16 [8192, 1024], P('seq'), may hold values from -6 to 6
- norm1_gain: float32 [1024], replicated, may hold values from 0.25 to 1.75
- w_query: bfloat16 [1024, 1024], P(None, 'tp'), may hold values from -3 to 3
- w_key: bfloat16 [1024, 512], P(None, 'tp'), may hold values from -2 to 2
- w_value: bfloat16 [1024, 512], P(None, 'tp'), may hold values from -0.1875 to 0.1875
- w_out: bfloat16 [1024, 1024], P('tp'), may hold values from -0.1875 to 0.1875
- norm2_gain: float32 [1024], replicated, may hold values from 0.25 to 1.75
- w_gate: bfloat16 [32, 1024, 512], P('seq'), may hold values from -0.1875 to 0.1875
- w_up: bfloat16 [32, 1024, 512], P('seq'), may hold values from -0.1875 to 0.1875
- w_down: bfloat16 [32, 512, 1024], P('seq'), may hold values from -0.25 to 0.25
- cache_in: bfloat16 [288, 256, 8, 128], P('seq', None, 'tp'), may hold values from -48 to 48
- cache_len: int32 [4], replicated, may hold values from 0 to 16384, as said below
- block_table: int32 [288], replicated, may hold values from 0 to 287, each once
- routes: int32 [8192, 8], P(('seq', 'tp')), may hold values from 0 to 31, all different within a row; in each aligned block of 32 rows (0 to 31, 32 to 63, ...) at most 12 rows name the same one
- gate_w: float32 [8192, 8], P(('seq', 'tp')), may hold values from 0.05 to 0.35
Outputs:
- hidden_out: bfloat16 [8192, 1024], P(('seq', 'tp'))
- cache_out: bfloat16 [288, 256, 8, 128], P('seq', None, 'tp')
Inputs may be any that keep to these rules, and one draw needn't show every extreme that they name: `cache_len`: some request holds exactly 16384 entries. `block_table`: each pool block appears once; pool block b lies on index b // 9 of seq. `routes`: each row names 8 different experts; among the rows of one device (aligned blocks of 32 rows) no expert is named more than 12 times, a bound that some block reaches.
All inputs are finite; a program needn't handle non-finite values.
Results may differ from a plain program's by a relative error of at most 0.035.
The roundings to bfloat16 on the way count: a program that leaves them out, or rounds other values in their place, can miss the bound.
Values may be sent and summed in bfloat16 or wider, within the bound.
No kernel may reach another device: no remote copies, remote signals or barrier semaphores. Data moves between devices by JAX's collectives and lax.ppermute only.
A program may use at most 128 MiB of HBM per device.

v0:
```python
import math
import jax
import jax.numpy as jnp
from jax import lax
from jax.sharding import PartitionSpec as P

D = 1024
HD = 64
GROUP = 2
TOP = 8
STRETCH = 2048
BS = 256
TOK_DEV = 256
MAXB = 72
norm_eps = 1e-05
rope_base = 10000.0
mask_fill = -1e30


def rms_scale(inputs, gains):
    floats = inputs.astype(jnp.float32)
    mean_square = jnp.mean(floats * floats, axis=-1, keepdims=True)
    return (floats * lax.rsqrt(mean_square + norm_eps) * gains).astype(jnp.bfloat16)


def rotate(vectors, positions):
    halfway = vectors.shape[-1] // 2
    counter = jnp.arange(halfway, dtype=jnp.int32).astype(jnp.float32)
    frequency = jnp.exp(counter * (-2.0 * math.log(rope_base) / vectors.shape[-1]))
    angles = positions.astype(jnp.float32)[:, None] * frequency[None, :]
    cosine = jnp.cos(angles)[:, None, :]
    sine_part = jnp.sin(angles)[:, None, :]
    front_half = vectors[..., :halfway]
    back_half = vectors[..., halfway:]
    return jnp.concatenate(
        [front_half * cosine - back_half * sine_part, back_half * cosine + front_half * sine_part],
        axis=-1,
    )


def on_device(
    hidden,
    norm1_gain,
    w_query,
    w_key,
    w_value,
    w_out,
    norm2_gain,
    w_gate,
    w_up,
    w_down,
    cache_in,
    cache_len,
    block_table,
    routes,
    gate_w,
):
    seq_count = lax.axis_size("seq")
    seq_place = lax.axis_index("seq")
    tp_place = lax.axis_index("tp")
    scaling = 1.0 / math.sqrt(HD)
    token_ids = seq_place * TOK_DEV + jnp.arange(TOK_DEV, dtype=jnp.int32)
    offsets = token_ids % STRETCH
    positions = cache_len[token_ids // STRETCH] + offsets
    normed = rms_scale(hidden, norm1_gain)
    queries = jnp.dot(normed, w_query, preferred_element_type=jnp.float32).reshape(
        TOK_DEV, GROUP, HD
    )
    queries = rotate(queries, positions).astype(jnp.bfloat16)
    key_rows = jnp.dot(normed, w_key, preferred_element_type=jnp.float32).reshape(TOK_DEV, 1, HD)
    key_rows = rotate(key_rows, positions).reshape(TOK_DEV, HD).astype(jnp.bfloat16)
    value_rows = jnp.dot(normed, w_value, preferred_element_type=jnp.float32).astype(jnp.bfloat16)
    new_rows = jnp.concatenate([key_rows, value_rows], axis=1)
    flat_queries = queries.reshape(TOK_DEV, GROUP * HD)
    all_queries, all_rows = (
        lax.all_gather(flat_queries, "seq", axis=0, tiled=True),
        lax.all_gather(new_rows, "seq", axis=0, tiled=True),
    )
    query_total = all_queries.shape[0]
    blk_count = cache_in.shape[0]
    pool_size = block_table.shape[0]
    pool_ids = seq_place * blk_count + jnp.arange(blk_count, dtype=jnp.int32)
    matched = block_table[None, :] == pool_ids[:, None]
    slot_of = jnp.sum(
        jnp.where(matched, jnp.arange(pool_size, dtype=jnp.int32)[None, :], 0), axis=1
    )
    block_req = slot_of // MAXB
    block_pos = slot_of % MAXB * BS
    cache_layer = cache_in[:, :, 0, :]
    span_rows = STRETCH * GROUP

    def update(block_id, states):
        row_peak, row_mass, row_accum = states
        request = block_req[block_id]
        first_row = request * span_rows
        filled = cache_len[request]
        entries = cache_layer[block_id]
        span_queries = lax.dynamic_slice_in_dim(all_queries, request * STRETCH, STRETCH, 0).reshape(
            span_rows, HD
        )
        scores = (
            jnp.einsum(
                "qd,kd->qk", span_queries, entries[:, :HD], preferred_element_type=jnp.float32
            )
            * scaling
        )
        visible = block_pos[block_id] + jnp.arange(BS, dtype=jnp.int32) < filled
        scores = jnp.where(visible[None, :], scores, mask_fill)
        old_peak = lax.dynamic_slice_in_dim(row_peak, first_row, span_rows, 0)
        new_peak = jnp.maximum(old_peak, jnp.max(scores, axis=-1))
        weights = jnp.where(visible[None, :], jnp.exp(scores - new_peak[:, None]), 0.0)
        retain = jnp.exp(old_peak - new_peak)
        old_mass = lax.dynamic_slice_in_dim(row_mass, first_row, span_rows, 0)
        old_accum = lax.dynamic_slice_in_dim(row_accum, first_row, span_rows, 0)
        mixed = jnp.einsum(
            "qk,kd->qd",
            weights.astype(jnp.bfloat16),
            entries[:, HD:],
            preferred_element_type=jnp.float32,
        )
        row_peak = lax.dynamic_update_slice_in_dim(row_peak, new_peak, first_row, 0)
        row_mass = lax.dynamic_update_slice_in_dim(
            row_mass, old_mass * retain + jnp.sum(weights, axis=-1), first_row, 0
        )
        row_accum = lax.dynamic_update_slice_in_dim(
            row_accum, old_accum * retain[:, None] + mixed, first_row, 0
        )
        return (row_peak, row_mass, row_accum)

    def visit_block(block_id, states):
        return update(block_id, states)

    flat_total = query_total * GROUP
    start_states = (
        jnp.full((flat_total,), mask_fill, jnp.float32),
        jnp.zeros((flat_total,), jnp.float32),
        jnp.zeros((flat_total, HD), jnp.float32),
    )
    row_peak, row_mass, row_accum = lax.fori_loop(0, blk_count, visit_block, start_states)
    each_peak, each_mass, each_accum = (
        lax.all_to_all(
            row_peak.reshape(seq_count, TOK_DEV * GROUP),
            "seq",
            split_axis=0,
            concat_axis=0,
            tiled=True,
        ),
        lax.all_to_all(
            row_mass.reshape(seq_count, TOK_DEV * GROUP),
            "seq",
            split_axis=0,
            concat_axis=0,
            tiled=True,
        ),
        lax.all_to_all(
            row_accum.reshape(seq_count, TOK_DEV, GROUP * HD),
            "seq",
            split_axis=0,
            concat_axis=0,
            tiled=True,
        ),
    )
    top_peak = jnp.max(each_peak, axis=0)
    factor = jnp.exp(each_peak - top_peak[None])
    got_mass = jnp.sum(each_mass * factor, axis=0).reshape(TOK_DEV, GROUP)
    got_accum = jnp.sum(
        each_accum.reshape(seq_count, TOK_DEV * GROUP, HD) * factor[..., None], axis=0
    ).reshape(TOK_DEV, GROUP, HD)
    my_peak = top_peak.reshape(TOK_DEV, GROUP)
    own_request = seq_place * TOK_DEV // STRETCH
    own_rows = lax.dynamic_slice_in_dim(all_rows, own_request * STRETCH, STRETCH, 0)
    own_queries = queries.reshape(TOK_DEV * GROUP, HD)
    self_scores = (
        jnp.einsum("qd,kd->qk", own_queries, own_rows[:, :HD], preferred_element_type=jnp.float32)
        * scaling
    )
    row_offsets = jnp.repeat(offsets, GROUP)
    causal = jnp.arange(STRETCH, dtype=jnp.int32)[None, :] <= row_offsets[:, None]
    self_scores = jnp.where(causal, self_scores, mask_fill)
    self_peak = jnp.max(self_scores, axis=-1)
    self_weights = jnp.where(causal, jnp.exp(self_scores - self_peak[:, None]), 0.0)
    self_mass = jnp.sum(self_weights, axis=-1).reshape(TOK_DEV, GROUP)
    self_accum = jnp.einsum(
        "qk,kd->qd",
        self_weights.astype(jnp.bfloat16),
        own_rows[:, HD:],
        preferred_element_type=jnp.float32,
    ).reshape(TOK_DEV, GROUP, HD)
    self_peak = self_peak.reshape(TOK_DEV, GROUP)
    final_peak = jnp.maximum(my_peak, self_peak)
    cache_share = jnp.exp(my_peak - final_peak)
    self_share = jnp.exp(self_peak - final_peak)
    denom = got_mass * cache_share + self_mass * self_share
    attention = (got_accum * cache_share[..., None] + self_accum * self_share[..., None]) / denom[
        ..., None
    ]
    attention = attention.reshape(TOK_DEV, GROUP * HD).astype(jnp.bfloat16)
    tp_rows = TOK_DEV // lax.axis_size("tp")
    head_total = lax.psum_scatter(
        jnp.dot(attention, w_out, preferred_element_type=jnp.float32).astype(jnp.bfloat16),
        "tp",
        scatter_dimension=0,
        tiled=True,
    ).astype(jnp.float32)
    own_hidden = lax.dynamic_slice_in_dim(hidden, tp_place * tp_rows, tp_rows, 0)
    residual = (own_hidden.astype(jnp.float32) + head_total).astype(jnp.bfloat16)
    normed2 = rms_scale(residual, norm2_gain)
    capacity = min(tp_rows, 3 * tp_rows * TOP // (2 * seq_count))
    flat_expert = routes.reshape(tp_rows * TOP)
    onehot = (flat_expert[:, None] == jnp.arange(seq_count, dtype=jnp.int32)[None, :]).astype(
        jnp.int32
    )
    ranking = jnp.sum((jnp.cumsum(onehot, axis=0) - onehot) * onehot, axis=1)
    slot_ids = flat_expert * capacity + ranking
    sources = jnp.arange(tp_rows * TOP, dtype=jnp.int32) // TOP
    table = jnp.zeros((seq_count * capacity,), jnp.int32).at[slot_ids].set(sources)
    occupied = jnp.zeros((seq_count * capacity,), jnp.bool_).at[slot_ids].set(True)
    outgoing = jnp.where(occupied[:, None], normed2[table], jnp.zeros((), jnp.bfloat16)).reshape(
        seq_count, capacity, D
    )
    incoming = lax.all_to_all(outgoing, "seq", split_axis=0, concat_axis=0, tiled=True)
    senders = incoming.shape[0]
    items = incoming.shape[1]
    flat_rows = incoming.reshape(senders * items, D)
    gate_part = jnp.dot(flat_rows, w_gate[0], preferred_element_type=jnp.float32)
    up_part = jnp.dot(flat_rows, w_up[0], preferred_element_type=jnp.float32)
    inner = (jax.nn.silu(gate_part) * up_part).astype(jnp.bfloat16)
    answer = jnp.dot(inner, w_down[0], preferred_element_type=jnp.float32).astype(jnp.bfloat16)
    answered = answer.reshape(senders, items, D)
    returned = lax.all_to_all(answered, "seq", split_axis=0, concat_axis=0, tiled=True)
    picked = returned.reshape(seq_count * capacity, D)[slot_ids].reshape(tp_rows, TOP, D)
    expert_sum = jnp.sum(gate_w[..., None] * picked.astype(jnp.float32), axis=1)
    hidden_out = (residual.astype(jnp.float32) + expert_sum).astype(jnp.bfloat16)
    block_offsets = block_pos[:, None] + jnp.arange(BS, dtype=jnp.int32)[None, :]
    block_fill = cache_len[block_req][:, None]
    inside = (block_offsets >= block_fill) & (block_offsets < block_fill + STRETCH)
    source_rows = block_req[:, None] * STRETCH + jnp.clip(
        block_offsets - block_fill, 0, STRETCH - 1
    )
    fresh = all_rows[source_rows]
    cache_out = jnp.where(inside[..., None], fresh, cache_layer)[:, :, None, :]
    return (hidden_out, cache_out)


def solution(mesh):
    placed = (
        P("seq", None),
        P(),
        P(None, "tp"),
        P(None, "tp"),
        P(None, "tp"),
        P("tp", None),
        P(),
        P("seq", None, None),
        P("seq", None, None),
        P("seq", None, None),
        P("seq", None, "tp", None),
        P(),
        P(),
        P(("seq", "tp"), None),
        P(("seq", "tp"), None),
    )
    return jax.shard_map(
        on_device,
        mesh=mesh,
        in_specs=placed,
        out_specs=(P(("seq", "tp"), None), P("seq", None, "tp", None)),
        check_vma=False,
    )
```

profile of v0, /device:TPU:1, one launch (start us, length us, event | category | flops | bytes accessed | tf_op | source)
XLA Modules:
  0.0 443.7 jit_solution(978709974458189872)
XLA Ops:
  19.0 49.9 %all-gather.3.cloned.1.call-done = bf16[8192,128]{0,1:T(8,128)(2,1)} async-done(((bf16[256,128]{0,1:T(8,128)(2,1)}), bf16[8192,128]{0,1:T(8,128)(2,1)}) %all-gather.3.cloned.1.call-update) | async-done | bytes 2097168 | tf_op jit(solution)/shard_map/all_gather | solution.py:76
  71.8 170.7 %while.17 = (s32[]{:T(128)}, f32[16384]{0:T(1024)S(1)}, f32[16384]{0:T(1024)}, f32[16384,64]{0,1:T(8,128)}, s32[9]{0:T(128)S(1)}, /*index=5*/s32[9]{0:T(128)S(1)...) while((s32[]{:T(128)}, f32[16384]{0:T(1024)S(1)}, ...), condition=%wide.region_5.6_spmd, body=%wide.region_2.5_spmd.sunk | while | flops 278405632 | bytes 35898736 | solution.py:139
  79.9 2.6 fusion.101
  83.2 3.2 fusion.103
  87.7 3.1 fusion.104
  98.9 2.6 fusion.101
  102.2 3.1 fusion.103
  106.7 3.1 fusion.104
  117.9 2.6 fusion.101
  121.2 3.1 fusion.103
  125.7 3.1 fusion.104
  140.1 3.1 fusion.103
  144.6 3.1 fusion.104
  155.9 2.6 fusion.101
  159.1 3.1 fusion.103
  163.6 3.1 fusion.104
  174.8 2.6 fusion.101
  178.1 3.1 fusion.103
  182.6 3.1 fusion.104
  193.8 2.6 fusion.101
  197.1 3.1 fusion.103
  201.5 3.1 fusion.104
  212.7 2.6 fusion.101
  216.0 3.1 fusion.103
  220.5 3.1 fusion.104
  231.7 2.6 fusion.101
  234.9 3.1 fusion.103
  239.4 3.1 fusion.104
  242.6 12.3 %all_to_all.39 = f32[32,1,512]{2,1,0:T(1,128)S(1)} all-to-all(f32[32,1,512]{2,1,0:T(1,128)S(1)} %bitcast.101), channel_id=1, replica_groups=mesh['seq'=32,'tp'=8] {'seq'}, dimensions={0} | all-to-all | bytes 131072 | tf_op jit(solution)/shard_map/all_to_all | solution.py:141
  254.9 3.9 all-to-all-start.2
  258.8 6.9 %copy.74 = f32[16384,64]{1,0:T(8,128)} copy(f32[16384,64]{0,1:T(8,128)} %get-tuple-element.158) | data formatting | bytes 8388608 | tf_op jit(solution)/shard_map/while | solution.py:139
  265.7 7.2 %reshape.606 = f32[32,256,128]{2,1,0:T(8,128)} reshape(f32[16384,64]{1,0:T(8,128)} %copy.74) | data formatting | bytes 8388608 | tf_op jit(solution)/shard_map/reshape | solution.py:156
  272.9 7.7 %all-to-all-start = ((f32[32,256,128]{2,1,0:T(8,128)}), f32[32,256,128]{2,1,0:T(8,128)}, u32[]{:S(2)}, u32[]{:S(2)}) async-start(f32[32,256,128]{2,1,0:T(8,128)} %reshape.606), calls=%async_computation | async-start | bytes 8388608 | tf_op jit(solution)/shard_map/all_to_all | solution.py:155
  282.2 3.8 fusion.11
  286.1 3.5 fusion.12
  289.9 3.4 fusion.14
  293.7 4.5 %mul.312 = f32[32,512,64]{2,1,0:T(8,128)} broadcast(f32[32,512]{1,0:T(8,128)S(1)} %get-tuple-element.228), dimensions={0,1} | broadcast | bytes 4259840 | tf_op jit(solution)/shard_map/mul | solution.py:167
  298.3 7.2 %mul.313 = f32[32,256,128]{2,1,0:T(8,128)} reshape(f32[32,512,64]{2,1,0:T(8,128)} %mul.312) | data formatting | bytes 8388608 | tf_op jit(solution)/shard_map/mul | solution.py:167
  306.2 26.5 %all-to-all-done = f32[32,256,128]{2,1,0:T(8,128)} async-done(((f32[32,256,128]{2,1,0:T(8,128)}), f32[32,256,128]{2,1,0:T(8,128)}, u32[]{:S(2)}, u32[]{:S(2)}) %all-to-all-start) | async-done | bytes 4194336 | tf_op jit(solution)/shard_map/all_to_all | solution.py:155
  332.7 3.9 multiply_reduce_fusion
  341.4 30.2 %reduce-scatter.2.cloned.1.call-done = bf16[32,1024]{1,0:T(8,128)(2,1)} async-done(((bf16[256,1024]{1,0:T(8,128)(2,1)}), bf16[32,1024]{1,0:T(8,128)(2,1)}) %reduce-scatter.2.cloned.1.call-update) | async-done | bytes 65552 | tf_op jit(solution)/shard_map/reduce_scatter | solution.py:199
  376.1 12.3 %all-to-all-start.3 = ((bf16[32,12,1024]{2,1,0:T(8,128)(2,1)}), bf16[32,12,1024]{2,1,0:T(8,128)(2,1)S(1)}, u32[]{:S(2)}, u32[]{:S(2)}) async-start(bf16[32,12,1024]{2,1,0:T(8,128)(2,1)} %broadcast_select_fusion), calls=%async_computation.4 | async-start | bytes 2097152 | tf_op jit(solution)/shard_map/all_to_all | solution.py:221
  389.2 16.1 %all-to-all-done.3 = bf16[32,12,1024]{2,1,0:T(8,128)(2,1)S(1)} async-done(((bf16[32,12,1024]{2,1,0:T(8,128)(2,1)}), bf16[32,12,1024]{2,1,0:T(8,128)(2,1)S(1)}, u32[]{:S(2)}, u32[]{:S(2)}) %all-to-all-start.3) | async-done | bytes 786464 | tf_op jit(solution)/shard_map/all_to_all | solution.py:221
  405.5 2.7 fusion.24
  412.0 4.7 %all-to-all-start.4 = ((bf16[32,12,1024]{2,1,0:T(8,128)(2,1)}), bf16[32,12,1024]{2,1,0:T(8,128)(2,1)}, u32[]{:S(2)}, u32[]{:S(2)}) async-start(bf16[32,12,1024]{2,1,0:T(8,128)(2,1)} %reshape.615), calls=%async_computation.5 | async-start | bytes 2097152 | tf_op jit(solution)/shard_map/all_to_all | solution.py:230
  416.9 3.2 copy.92
  420.1 5.6 %gather_fusion.3 = bf16[2304,128]{1,0:T(8,128)(2,1)} fusion(bf16[8192,128]{1,0:T(8,128)(2,1)S(1)} %copy.92, s32[3072]{0:T(1024)S(1)} %pad_clamp_fusion), kind=kCustom, calls=%fused_computation.3 | custom fusion | bytes 1188864 | tf_op jit(solution)/shard_map/gather | solution.py:240
  427.9 5.7 %all-to-all-done.4 = bf16[32,12,1024]{2,1,0:T(8,128)(2,1)} async-done(((bf16[32,12,1024]{2,1,0:T(8,128)(2,1)}), bf16[32,12,1024]{2,1,0:T(8,128)(2,1)}, u32[]{:S(2)}, u32[]{:S(2)}) %all-to-all-start.4) | async-done | bytes 786464 | tf_op jit(solution)/shard_map/all_to_all | solution.py:230
  (237 shorter events, 104.1 us)
Async XLA Ops:
  7.2 401.0 %copy-start = (bf16[1,512,1024]{2,1,0:T(8,128)(2,1)S(1)}, bf16[1,512,1024]{2,1,0:T(8,128)(2,1)}, u32[]{:S(2)}) copy-start(bf16[1,512,1024]{2,1,0:T(8,128)(2,1)} %param.26) | copy-start | bytes 3145732
  7.2 11.6 %copy-start.7 = (s32[288]{0:T(512)S(1)}, s32[288]{0:T(512)}, u32[]{:S(2)}) copy-start(s32[288]{0:T(512)} %param.29) | copy-start | bytes 3460
  7.2 61.7 %all-gather.3.cloned.1.call-start = ((), (), s32[]{:S(2)}) async-start(), calls=%async_computation.6 | async-start | bytes 2162688 | tf_op jit(solution)/shard_map/all_gather | solution.py:76
  12.8 59.1 %copy-start.2 = (s32[4]{0:T(128)S(1)}, s32[4]{0:T(128)}, u32[]{:S(2)}) copy-start(s32[4]{0:T(128)} %param.28) | copy-start | bytes 52
  15.0 267.2 %all-gather.5.cloned.1.call-start = ((), (), s32[]{:S(2)}) async-start(), calls=%async_computation.7 | async-start | bytes 2162688 | tf_op jit(solution)/shard_map/all_gather | solution.py:77
  83.1 4.6 %copy-start.1 = (f32[4096,256]{0,1:T(8,128)S(1)}, f32[4096,256]{0,1:T(8,128)}, u32[]{:S(2)}) copy-start(f32[4096,256]{0,1:T(8,128)} %get-tuple-element.309) | copy-start | bytes 12582916 | tf_op jit(solution)/shard_map/while
  102.1 4.5 %copy-start.1 = (f32[4096,256]{0,1:T(8,128)S(1)}, f32[4096,256]{0,1:T(8,128)}, u32[]{:S(2)}) copy-start(f32[4096,256]{0,1:T(8,128)} %get-tuple-element.309) | copy-start | bytes 12582916 | tf_op jit(solution)/shard_map/while
  121.1 4.5 %copy-start.1 = (f32[4096,256]{0,1:T(8,128)S(1)}, f32[4096,256]{0,1:T(8,128)}, u32[]{:S(2)}) copy-start(f32[4096,256]{0,1:T(8,128)} %get-tuple-element.309) | copy-start | bytes 12582916 | tf_op jit(solution)/shard_map/while
  140.1 4.5 %copy-start.1 = (f32[4096,256]{0,1:T(8,128)S(1)}, f32[4096,256]{0,1:T(8,128)}, u32[]{:S(2)}) copy-start(f32[4096,256]{0,1:T(8,128)} %get-tuple-element.309) | copy-start | bytes 12582916 | tf_op jit(solution)/shard_map/while
  159.1 4.5 %copy-start.1 = (f32[4096,256]{0,1:T(8,128)S(1)}, f32[4096,256]{0,1:T(8,128)}, u32[]{:S(2)}) copy-start(f32[4096,256]{0,1:T(8,128)} %get-tuple-element.309) | copy-start | bytes 12582916 | tf_op jit(solution)/shard_map/while
  178.1 4.5 %copy-start.1 = (f32[4096,256]{0,1:T(8,128)S(1)}, f32[4096,256]{0,1:T(8,128)}, u32[]{:S(2)}) copy-start(f32[4096,256]{0,1:T(8,128)} %get-tuple-element.309) | copy-start | bytes 12582916 | tf_op jit(solution)/shard_map/while
  197.0 4.5 %copy-start.1 = (f32[4096,256]{0,1:T(8,128)S(1)}, f32[4096,256]{0,1:T(8,128)}, u32[]{:S(2)}) copy-start(f32[4096,256]{0,1:T(8,128)} %get-tuple-element.309) | copy-start | bytes 12582916 | tf_op jit(solution)/shard_map/while
  216.0 4.5 %copy-start.1 = (f32[4096,256]{0,1:T(8,128)S(1)}, f32[4096,256]{0,1:T(8,128)}, u32[]{:S(2)}) copy-start(f32[4096,256]{0,1:T(8,128)} %get-tuple-element.309) | copy-start | bytes 12582916 | tf_op jit(solution)/shard_map/while
  234.9 4.5 %copy-start.1 = (f32[4096,256]{0,1:T(8,128)S(1)}, f32[4096,256]{0,1:T(8,128)}, u32[]{:S(2)}) copy-start(f32[4096,256]{0,1:T(8,128)} %get-tuple-element.309) | copy-start | bytes 12582916 | tf_op jit(solution)/shard_map/while
  254.9 18.0 %all-to-all-start.2 = ((f32[32,1,512]{2,1,0:T(1,128)}), f32[32,1,512]{2,1,0:T(1,128)S(1)}, u32[]{:S(2)}, u32[]{:S(2)}) async-start(f32[32,1,512]{2,1,0:T(1,128)} %bitcast.19), calls=%async_computation.2 | async-start | bytes 131072 | tf_op jit(solution)/shard_map/all_to_all | solution.py:148
  272.9 8.4 %copy-start.4 = (s32[32,8]{0,1:T(8,128)S(1)}, s32[32,8]{0,1:T(8,128)}, u32[]{:S(2)}) copy-start(s32[32,8]{0,1:T(8,128)} %param.30) | copy-start | bytes 3076
  272.9 59.8 %all-to-all-start = ((f32[32,256,128]{2,1,0:T(8,128)}), f32[32,256,128]{2,1,0:T(8,128)}, u32[]{:S(2)}, u32[]{:S(2)}) async-start(f32[32,256,128]{2,1,0:T(8,128)} %reshape.606), calls=%async_computation | async-start | bytes 8388608 | tf_op jit(solution)/shard_map/all_to_all | solution.py:155
  280.6 91.0 %reduce-scatter.2.cloned.1.call-start = ((), (), s32[]{:S(2)}) async-start(), calls=%async_computation.8 | async-start | bytes 589824 | tf_op jit(solution)/shard_map/reduce_scatter | solution.py:199
  306.2 30.4 %copy-start.3 = (bf16[128,1024]{1,0:T(8,128)(2,1)S(1)}, bf16[128,1024]{1,0:T(8,128)(2,1)}, u32[]{:S(2)}) copy-start(bf16[128,1024]{1,0:T(8,128)(2,1)} %param.22) | copy-start | bytes 786436
  306.2 66.4 %copy-start.5 = (f32[1024]{0:T(1024)S(1)}, f32[1024]{0:T(1024)}, u32[]{:S(2)}) copy-start(f32[1024]{0:T(1024)} %param.23) | copy-start | bytes 12292
  376.1 29.2 %all-to-all-start.3 = ((bf16[32,12,1024]{2,1,0:T(8,128)(2,1)}), bf16[32,12,1024]{2,1,0:T(8,128)(2,1)S(1)}, u32[]{:S(2)}, u32[]{:S(2)}) async-start(bf16[32,12,1024]{2,1,0:T(8,128)(2,1)} %broadcast_select_fusion), calls=%async_computation.4 | async-start | bytes 2097152 | tf_op jit(solution)/shard_map/all_to_all | solution.py:221
  408.2 8.5 %copy-start.6 = (f32[32,8]{0,1:T(8,128)S(1)}, f32[32,8]{0,1:T(8,128)}, u32[]{:S(2)}) copy-start(f32[32,8]{0,1:T(8,128)} %param.31) | copy-start | bytes 3076
  412.0 21.6 %all-to-all-start.4 = ((bf16[32,12,1024]{2,1,0:T(8,128)(2,1)}), bf16[32,12,1024]{2,1,0:T(8,128)(2,1)}, u32[]{:S(2)}, u32[]{:S(2)}) async-start(bf16[32,12,1024]{2,1,0:T(8,128)(2,1)} %reshape.615), calls=%async_computation.5 | async-start | bytes 2097152 | tf_op jit(solution)/shard_map/all_to_all | solution.py:230
Sparse Core Ops, SparseCore 0:
  15.1 53.7 all-gather.2
  71.9 49.0 all-gather.4
  337.8 33.6 reduce-scatter.1
where the time goes:
time: 447 us; the launch traced here: 444 us
  waiting for transfers between devices  128 us (29%)
  local copies, waits for them, and re-layouts  91.9 us (21%)
  other arithmetic  71.6 us (16%)
  matrix products  69.7 us (16%)
  starting transfers between devices  28.9 us (6%)
  loops' own time  26.6 us (6%)
  between operations  14.3 us (3%)
  blocking collectives  12.3 us (3%)
    all_gather x1, waiting for transfers between devices, on_device(): lax.all_gather(flat_queries, 'seq', axis=0, tiled=True)  49.9 us
    reduce_scatter x1, waiting for transfers between devices, on_device(): lax.psum_scatter(jnp.dot(attention, w_out, preferred_element_type=jnp.flo...  30.2 us
    reduce_sum x9, other arithmetic, update(): jnp.sum(weights, axis=-1)  28.2 us
    dot_general x9, matrix products, update(): jnp.einsum('qk,kd->qd', weights.astype(jnp.bfloat16), entries[:, HD:], pr...  28.1 us
    another operation x1, loops' own time, on_device(): lax.fori_loop(0, blk_count, visit_block, start_states)  26.6 us
    all_to_all x1, waiting for transfers between devices, on_device(): lax.all_to_all(row_accum.reshape(seq_count, TOK_DEV, GROUP * HD), 'seq',...  26.5 us
    dot_general x9, matrix products, update(): jnp.einsum('qd,kd->qk', span_queries, entries[:, :HD], preferred_element_...  23.7 us
    all_to_all x1, waiting for transfers between devices, on_device(): lax.all_to_all(outgoing, 'seq', split_axis=0, concat_axis=0, tiled=True)  16.1 us
  transfers between devices with their start and end apart: 7, of which 5 were waited for; matrix products, arithmetic and copies ran while one was open for 46% of the time, Pallas kernels for 0%

commit v1 on v0

--- a/solution.py
+++ b/solution.py
@@ -73,7 +73,9 @@
     new_rows = jnp.concatenate([key_rows, value_rows], axis=1)
     flat_queries = queries.reshape(TOK_DEV, GROUP * HD)
     all_queries, all_rows = (
-        lax.all_gather(flat_queries, "seq", axis=0, tiled=True),
+        jnp.concatenate(
+            lax.all_to_all(jnp.stack([flat_queries] * lax.axis_size("seq")), "seq", 0, 0), axis=0
+        ),
         lax.all_gather(new_rows, "seq", axis=0, tiled=True),
     )
     query_total = all_queries.shape[0]

time: 447 us -> 430 us (0.962)
  waiting for transfers between devices: 128 us -> 107 us
  starting transfers between devices: 28.9 us -> 37.4 us
    all_gather x1 -> x0, waiting for transfers between devices: 49.9 us -> none  [on_device(): lax.all_gather(flat_queries, 'seq', axis=0, tiled=True)]
    all_to_all x0 -> x1, waiting for transfers between devices: none -> 26.5 us  [on_device(): lax.all_to_all(jnp.stack([flat_queries] * lax.axis_size('seq')), 'seq', 0...]
    all_to_all x0 -> x1, starting transfers between devices: none -> 8.63 us  [on_device(): lax.all_to_all(jnp.stack([flat_queries] * lax.axis_size('seq')), 'seq', 0...]
    dynamic_slice x18 -> x9, local copies, waits for them, and re-layouts: 12.4 us -> 9.73 us  [update(): lax.dynamic_slice_in_dim(all_queries, request * STRETCH, STRETCH, 0)]
  transfers between devices with their start and end apart: 7 -> 7, of which waited for: 5 -> 5; matrix products, arithmetic and copies ran while one was open for 46% -> 47% of each run, Pallas kernels for 0% -> 0%
where the time goes in v1:
time: 430 us; the launch traced here: 426 us
  waiting for transfers between devices  107 us (25%)
  local copies, waits for them, and re-layouts  91.2 us (21%)
  other arithmetic  70.9 us (16%)
  matrix products  67.5 us (16%)
  starting transfers between devices  37.4 us (9%)
  loops' own time  26.5 us (6%)
  between operations  14.6 us (3%)
  blocking collectives  11.6 us (3%)
    reduce_scatter x1, waiting for transfers between devices, on_device(): lax.psum_scatter(jnp.dot(attention, w_out, preferred_element_type=jnp.flo...  31.8 us
    reduce_sum x9, other arithmetic, update(): jnp.sum(weights, axis=-1)  28.2 us
    dot_general x9, matrix products, update(): jnp.einsum('qk,kd->qd', weights.astype(jnp.bfloat16), entries[:, HD:], pr...  28 us
    all_to_all x1, waiting for transfers between devices, on_device(): lax.all_to_all(jnp.stack([flat_queries] * lax.axis_size('seq')), 'seq', 0...  26.5 us
    all_to_all x1, waiting for transfers between devices, on_device(): lax.all_to_all(row_accum.reshape(seq_count, TOK_DEV, GROUP * HD), 'seq',...  26.5 us
    another operation x1, loops' own time, on_device(): lax.fori_loop(0, blk_count, visit_block, start_states)  26.5 us
    dot_general x9, matrix products, update(): jnp.einsum('qd,kd->qk', span_queries, entries[:, :HD], preferred_element_...  23.7 us
    all_to_all x1, waiting for transfers between devices, on_device(): lax.all_to_all(outgoing, 'seq', split_axis=0, concat_axis=0, tiled=True)  16.1 us
  transfers between devices with their start and end apart: 7, of which 5 were waited for; matrix products, arithmetic and copies ran while one was open for 47% of the time, Pallas kernels for 0%

profile of v1, /device:TPU:1, one launch (start us, length us, event | category | flops | bytes accessed | tf_op | source)
XLA Modules:
  0.0 426.5 jit_solution(17631041410842052886)
XLA Ops:
  16.3 8.6 %all-to-all-start = ((bf16[32,256,128]{2,1,0:T(8,128)(2,1)}), bf16[32,256,128]{2,1,0:T(8,128)(2,1)}, u32[]{:S(2)}, u32[]{:S(2)}) async-start(bf16[32,256,128]{2,1,0:T(8,128)(2,1)} %stack.3), calls=%async_computation | async-start | bytes 4194304 | tf_op jit(solution)/shard_map/all_to_all | solution.py:77
  26.9 26.5 %all-to-all-done = bf16[32,256,128]{2,1,0:T(8,128)(2,1)} async-done(((bf16[32,256,128]{2,1,0:T(8,128)(2,1)}), bf16[32,256,128]{2,1,0:T(8,128)(2,1)}, u32[]{:S(2)}, u32[]{:S(2)}) %all-to-all-start) | async-done | bytes 2097184 | tf_op jit(solution)/shard_map/all_to_all | solution.py:77
  56.3 167.9 %while.17 = (s32[]{:T(128)}, f32[16384]{0:T(1024)S(1)}, f32[16384]{0:T(1024)}, f32[16384,64]{0,1:T(8,128)}, s32[9]{0:T(128)S(1)}, /*index=5*/s32[9]{0:T(128)S(1)...) while((s32[]{:T(128)}, f32[16384]{0:T(1024)S(1)}, ...), condition=%wide.region_5.6_spmd, body=%wide.region_2.5_spmd.sunk | while | flops 278405632 | bytes 34850160 | solution.py:141
  64.1 2.6 fusion.101
  67.4 3.1 fusion.103
  71.9 3.1 fusion.104
  82.8 2.6 fusion.101
  86.0 3.1 fusion.103
  90.5 3.1 fusion.104
  101.4 2.6 fusion.101
  104.7 3.1 fusion.103
  109.2 3.1 fusion.104
  123.4 3.1 fusion.103
  127.8 3.1 fusion.104
  138.8 2.6 fusion.101
  142.0 3.1 fusion.103
  146.5 3.1 fusion.104
  157.5 2.6 fusion.101
  160.7 3.1 fusion.103
  165.2 3.1 fusion.104
  176.1 2.6 fusion.101
  179.4 3.1 fusion.103
  183.9 3.1 fusion.104
  194.7 2.6 fusion.101
  198.0 3.1 fusion.103
  202.5 3.1 fusion.104
  216.6 3.1 fusion.103
  221.1 3.1 fusion.104
  224.3 11.6 %all_to_all.44 = f32[32,1,512]{2,1,0:T(1,128)S(1)} all-to-all(f32[32,1,512]{2,1,0:T(1,128)S(1)} %bitcast.102), channel_id=1, replica_groups=mesh['seq'=32,'tp'=8] {'seq'}, dimensions={0} | all-to-all | bytes 131072 | tf_op jit(solution)/shard_map/all_to_all | solution.py:143
  235.8 3.9 all-to-all-start.3
  239.7 6.9 %copy.89 = f32[16384,64]{1,0:T(8,128)} copy(f32[16384,64]{0,1:T(8,128)} %get-tuple-element.158) | data formatting | bytes 8388608 | tf_op jit(solution)/shard_map/while | solution.py:141
  246.6 7.2 %reshape.611 = f32[32,256,128]{2,1,0:T(8,128)} reshape(f32[16384,64]{1,0:T(8,128)} %copy.89) | data formatting | bytes 8388608 | tf_op jit(solution)/shard_map/reshape | solution.py:158
  253.9 7.7 %all-to-all-start.1 = ((f32[32,256,128]{2,1,0:T(8,128)}), f32[32,256,128]{2,1,0:T(8,128)}, u32[]{:S(2)}, u32[]{:S(2)}) async-start(f32[32,256,128]{2,1,0:T(8,128)} %reshape.611), calls=%async_computation.1 | async-start | bytes 8388608 | tf_op jit(solution)/shard_map/all_to_all | solution.py:157
  263.4 4.5 %mul.312 = f32[32,512,64]{2,1,0:T(8,128)} broadcast(f32[32,512]{1,0:T(8,128)S(1)} %get-tuple-element.192), dimensions={0,1} | broadcast | bytes 4259840 | tf_op jit(solution)/shard_map/mul | solution.py:169
  267.9 7.2 %mul.313 = f32[32,256,128]{2,1,0:T(8,128)} reshape(f32[32,512,64]{2,1,0:T(8,128)} %mul.312) | data formatting | bytes 8388608 | tf_op jit(solution)/shard_map/mul | solution.py:169
  275.5 3.8 fusion.11
  279.4 3.5 fusion.12
  283.6 3.4 fusion.14
  287.2 26.5 %all-to-all-done.1 = f32[32,256,128]{2,1,0:T(8,128)} async-done(((f32[32,256,128]{2,1,0:T(8,128)}), f32[32,256,128]{2,1,0:T(8,128)}, u32[]{:S(2)}, u32[]{:S(2)}) %all-to-all-start.1) | async-done | bytes 4194336 | tf_op jit(solution)/shard_map/all_to_all | solution.py:157
  313.7 3.9 multiply_reduce_fusion
  322.3 31.8 %reduce-scatter.2.cloned.1.call-done = bf16[32,1024]{1,0:T(8,128)(2,1)} async-done(((bf16[256,1024]{1,0:T(8,128)(2,1)}), bf16[32,1024]{1,0:T(8,128)(2,1)}) %reduce-scatter.2.cloned.1.call-update) | async-done | bytes 65552 | tf_op jit(solution)/shard_map/reduce_scatter | solution.py:201
  358.6 12.3 %all-to-all-start.4 = ((bf16[32,12,1024]{2,1,0:T(8,128)(2,1)}), bf16[32,12,1024]{2,1,0:T(8,128)(2,1)S(1)}, u32[]{:S(2)}, u32[]{:S(2)}) async-start(bf16[32,12,1024]{2,1,0:T(8,128)(2,1)} %broadcast_select_fusion), calls=%async_computation.5 | async-start | bytes 2097152 | tf_op jit(solution)/shard_map/all_to_all | solution.py:223
  371.7 16.1 %all-to-all-done.4 = bf16[32,12,1024]{2,1,0:T(8,128)(2,1)S(1)} async-done(((bf16[32,12,1024]{2,1,0:T(8,128)(2,1)}), bf16[32,12,1024]{2,1,0:T(8,128)(2,1)S(1)}, u32[]{:S(2)}, u32[]{:S(2)}) %all-to-all-start.4) | async-done | bytes 786464 | tf_op jit(solution)/shard_map/all_to_all | solution.py:223
  388.0 2.7 fusion.24
  394.5 4.7 %all-to-all-start.5 = ((bf16[32,12,1024]{2,1,0:T(8,128)(2,1)}), bf16[32,12,1024]{2,1,0:T(8,128)(2,1)}, u32[]{:S(2)}, u32[]{:S(2)}) async-start(bf16[32,12,1024]{2,1,0:T(8,128)(2,1)} %reshape.620), calls=%async_computation.6 | async-start | bytes 2097152 | tf_op jit(solution)/shard_map/all_to_all | solution.py:232
  399.4 3.2 copy.107
  402.6 5.6 %gather_fusion.3 = bf16[2304,128]{1,0:T(8,128)(2,1)} fusion(bf16[8192,128]{1,0:T(8,128)(2,1)S(1)} %copy.107, s32[3072]{0:T(1024)S(1)} %pad_clamp_fusion), kind=kCustom, calls=%fused_computation.3 | custom fusion | bytes 1188864 | tf_op jit(solution)/shard_map/gather | solution.py:242
  410.4 5.7 %all-to-all-done.5 = bf16[32,12,1024]{2,1,0:T(8,128)(2,1)} async-done(((bf16[32,12,1024]{2,1,0:T(8,128)(2,1)}), bf16[32,12,1024]{2,1,0:T(8,128)(2,1)}, u32[]{:S(2)}, u32[]{:S(2)}) %all-to-all-start.5) | async-done | bytes 786464 | tf_op jit(solution)/shard_map/all_to_all | solution.py:232
  (237 shorter events, 103.2 us)
Async XLA Ops:
  7.2 383.5 %copy-start = (bf16[1,512,1024]{2,1,0:T(8,128)(2,1)S(1)}, bf16[1,512,1024]{2,1,0:T(8,128)(2,1)}, u32[]{:S(2)}) copy-start(bf16[1,512,1024]{2,1,0:T(8,128)(2,1)} %param.26) | copy-start | bytes 3145732
  11.3 13.8 %copy-start.3 = (bf16[256,1024]{1,0:T(8,128)(2,1)S(1)}, bf16[256,1024]{1,0:T(8,128)(2,1)}, u32[]{:S(2)}) copy-start(bf16[256,1024]{1,0:T(8,128)(2,1)} %param.17) | copy-start | bytes 1572868
  11.3 13.8 %copy-start.9 = (bf16[1024,64]{0,1:T(8,128)(2,1)S(1)}, bf16[1024,64]{0,1:T(8,128)(2,1)}, u32[]{:S(2)}) copy-start(bf16[1024,64]{0,1:T(8,128)(2,1)} %param.20) | copy-start | bytes 393220
  11.3 13.8 %copy-start.11 = (f32[1024]{0:T(1024)S(1)}, f32[1024]{0:T(1024)}, u32[]{:S(2)}) copy-start(f32[1024]{0:T(1024)} %param.18) | copy-start | bytes 12292
  14.3 11.3 %copy-start.10 = (bf16[1024,64]{0,1:T(8,128)(2,1)S(1)}, bf16[1024,64]{0,1:T(8,128)(2,1)}, u32[]{:S(2)}) copy-start(bf16[1024,64]{0,1:T(8,128)(2,1)} %param.21) | copy-start | bytes 393220
  14.5 12.2 %copy-start.8 = (s32[288]{0:T(512)S(1)}, s32[288]{0:T(512)}, u32[]{:S(2)}) copy-start(s32[288]{0:T(512)} %param.29) | copy-start | bytes 3460
  16.3 37.1 %all-to-all-start = ((bf16[32,256,128]{2,1,0:T(8,128)(2,1)}), bf16[32,256,128]{2,1,0:T(8,128)(2,1)}, u32[]{:S(2)}, u32[]{:S(2)}) async-start(bf16[32,256,128]{2,1,0:T(8,128)(2,1)} %stack.3), calls=%async_computation | async-start | bytes 4194304 | tf_op jit(solution)/shard_map/all_to_all | solution.py:77
  25.0 31.4 %copy-start.2 = (s32[4]{0:T(128)S(1)}, s32[4]{0:T(128)}, u32[]{:S(2)}) copy-start(s32[4]{0:T(128)} %param.28) | copy-start | bytes 52
  25.0 250.5 %all-gather.2.cloned.1.call-start = ((), (), s32[]{:S(2)}) async-start(), calls=%async_computation.7 | async-start | bytes 2162688 | tf_op jit(solution)/shard_map/all_gather | solution.py:79
  67.4 4.5 %copy-start.1 = (f32[4096,256]{0,1:T(8,128)S(1)}, f32[4096,256]{0,1:T(8,128)}, u32[]{:S(2)}) copy-start(f32[4096,256]{0,1:T(8,128)} %get-tuple-element.273) | copy-start | bytes 12582916 | tf_op jit(solution)/shard_map/while
  86.0 4.5 %copy-start.1 = (f32[4096,256]{0,1:T(8,128)S(1)}, f32[4096,256]{0,1:T(8,128)}, u32[]{:S(2)}) copy-start(f32[4096,256]{0,1:T(8,128)} %get-tuple-element.273) | copy-start | bytes 12582916 | tf_op jit(solution)/shard_map/while
  104.7 4.5 %copy-start.1 = (f32[4096,256]{0,1:T(8,128)S(1)}, f32[4096,256]{0,1:T(8,128)}, u32[]{:S(2)}) copy-start(f32[4096,256]{0,1:T(8,128)} %get-tuple-element.273) | copy-start | bytes 12582916 | tf_op jit(solution)/shard_map/while
  123.3 4.5 %copy-start.1 = (f32[4096,256]{0,1:T(8,128)S(1)}, f32[4096,256]{0,1:T(8,128)}, u32[]{:S(2)}) copy-start(f32[4096,256]{0,1:T(8,128)} %get-tuple-element.273) | copy-start | bytes 12582916 | tf_op jit(solution)/shard_map/while
  142.0 4.5 %copy-start.1 = (f32[4096,256]{0,1:T(8,128)S(1)}, f32[4096,256]{0,1:T(8,128)}, u32[]{:S(2)}) copy-start(f32[4096,256]{0,1:T(8,128)} %get-tuple-element.273) | copy-start | bytes 12582916 | tf_op jit(solution)/shard_map/while
  160.7 4.5 %copy-start.1 = (f32[4096,256]{0,1:T(8,128)S(1)}, f32[4096,256]{0,1:T(8,128)}, u32[]{:S(2)}) copy-start(f32[4096,256]{0,1:T(8,128)} %get-tuple-element.273) | copy-start | bytes 12582916 | tf_op jit(solution)/shard_map/while
  179.3 4.5 %copy-start.1 = (f32[4096,256]{0,1:T(8,128)S(1)}, f32[4096,256]{0,1:T(8,128)}, u32[]{:S(2)}) copy-start(f32[4096,256]{0,1:T(8,128)} %get-tuple-element.273) | copy-start | bytes 12582916 | tf_op jit(solution)/shard_map/while
  198.0 4.5 %copy-start.1 = (f32[4096,256]{0,1:T(8,128)S(1)}, f32[4096,256]{0,1:T(8,128)}, u32[]{:S(2)}) copy-start(f32[4096,256]{0,1:T(8,128)} %get-tuple-element.273) | copy-start | bytes 12582916 | tf_op jit(solution)/shard_map/while
  216.6 4.5 %copy-start.1 = (f32[4096,256]{0,1:T(8,128)S(1)}, f32[4096,256]{0,1:T(8,128)}, u32[]{:S(2)}) copy-start(f32[4096,256]{0,1:T(8,128)} %get-tuple-element.273) | copy-start | bytes 12582916 | tf_op jit(solution)/shard_map/while
  235.8 18.0 %all-to-all-start.3 = ((f32[32,1,512]{2,1,0:T(1,128)}), f32[32,1,512]{2,1,0:T(1,128)S(1)}, u32[]{:S(2)}, u32[]{:S(2)}) async-start(f32[32,1,512]{2,1,0:T(1,128)} %bitcast.20), calls=%async_computation.3 | async-start | bytes 131072 | tf_op jit(solution)/shard_map/all_to_all | solution.py:150
  253.9 8.4 %copy-start.5 = (s32[32,8]{0,1:T(8,128)S(1)}, s32[32,8]{0,1:T(8,128)}, u32[]{:S(2)}) copy-start(s32[32,8]{0,1:T(8,128)} %param.30) | copy-start | bytes 3076
  253.9 59.8 %all-to-all-start.1 = ((f32[32,256,128]{2,1,0:T(8,128)}), f32[32,256,128]{2,1,0:T(8,128)}, u32[]{:S(2)}, u32[]{:S(2)}) async-start(f32[32,256,128]{2,1,0:T(8,128)} %reshape.611), calls=%async_computation.1 | async-start | bytes 8388608 | tf_op jit(solution)/shard_map/all_to_all | solution.py:157
  261.6 92.6 %reduce-scatter.2.cloned.1.call-start = ((), (), s32[]{:S(2)}) async-start(), calls=%async_computation.8 | async-start | bytes 589824 | tf_op jit(solution)/shard_map/reduce_scatter | solution.py:201
  287.2 30.4 %copy-start.4 = (bf16[128,1024]{1,0:T(8,128)(2,1)S(1)}, bf16[128,1024]{1,0:T(8,128)(2,1)}, u32[]{:S(2)}) copy-start(bf16[128,1024]{1,0:T(8,128)(2,1)} %param.22) | copy-start | bytes 786436
  287.2 68.0 %copy-start.6 = (f32[1024]{0:T(1024)S(1)}, f32[1024]{0:T(1024)}, u32[]{:S(2)}) copy-start(f32[1024]{0:T(1024)} %param.23) | copy-start | bytes 12292
  358.6 29.2 %all-to-all-start.4 = ((bf16[32,12,1024]{2,1,0:T(8,128)(2,1)}), bf16[32,12,1024]{2,1,0:T(8,128)(2,1)S(1)}, u32[]{:S(2)}, u32[]{:S(2)}) async-start(bf16[32,12,1024]{2,1,0:T(8,128)(2,1)} %broadcast_select_fusion), calls=%async_computation.5 | async-start | bytes 2097152 | tf_op jit(solution)/shard_map/all_to_all | solution.py:223
  390.7 8.5 %copy-start.7 = (f32[32,8]{0,1:T(8,128)S(1)}, f32[32,8]{0,1:T(8,128)}, u32[]{:S(2)}) copy-start(f32[32,8]{0,1:T(8,128)} %param.31) | copy-start | bytes 3076
  394.5 21.6 %all-to-all-start.5 = ((bf16[32,12,1024]{2,1,0:T(8,128)(2,1)}), bf16[32,12,1024]{2,1,0:T(8,128)(2,1)}, u32[]{:S(2)}, u32[]{:S(2)}) async-start(bf16[32,12,1024]{2,1,0:T(8,128)(2,1)} %reshape.620), calls=%async_computation.6 | async-start | bytes 2097152 | tf_op jit(solution)/shard_map/all_to_all | solution.py:232
Sparse Core Ops, SparseCore 0:
  28.8 56.0 all-gather.1
  318.8 35.2 reduce-scatter.1
